TPU v7x, 512 devices: a whole 4x4x16 slice. The times are simulated.
512 devices in a mesh: dp: 16 (over x, y_hi, core), ctx: 32 (over y_lo, z).
Axes of the slice: x: 4, y: 4 (y_hi: 2, y_lo: 2; y = y_hi * 2 + y_lo), z: 16, core: 2. Of those that a mesh axis runs over, the one named last changes fastest.
Arguments:
- queries: bfloat16 [16, 4096, 2048], P('dp', 'ctx'), may hold values from -6 to 6
- keys: bfloat16 [16, 4096, 2048], P('dp', 'ctx'), may hold values from -6 to 6
- values: bfloat16 [16, 4096, 2048], P('dp', 'ctx'), may hold values from -6 to 6
- out_grad: bfloat16 [16, 4096, 2048], P('dp', 'ctx'), may hold values from -6 to 6
- out_proj: bfloat16 [2048, 2048], P('dp'), may hold values from -0.125 to 0.125
- attn_out: bfloat16 [16, 4096, 2048], P('dp', 'ctx'), may hold values from -3 to 3
- log_sum: float32 [16, 16, 4096], P('dp', None, 'ctx'), may hold values from 3 to 5
- group_order: int32 [16, 128], P('dp'), may hold values from 0 to 127, each once within a row
Outputs:
- query_grad: bfloat16 [16, 4096, 2048], P('dp', 'ctx')
- key_grad: bfloat16 [16, 4096, 2048], P('dp', 'ctx')
- value_grad: bfloat16 [16, 4096, 2048], P('dp', 'ctx')
Inputs may be any that keep to these rules, and one draw needn't show every extreme that they name: `group_order`: each row holds every number once.
All inputs are finite; a program needn't handle non-finite values.
Results may differ from a plain program's by a relative error of at most 0.0075.
Values may be sent and summed in bfloat16 or wider, within the bound.
A program may use at most 64 MiB of HBM per device.

v0:
```python
import jax
import jax.numpy as jnp
from jax import lax
from jax.sharding import PartitionSpec as P

GROUP = 32


def shifted(array, axis, by):
    size = lax.axis_size(axis)
    return lax.ppermute(array, axis, [(i, (i + by) % size) for i in range(size)])


def pair_grads(query_blk, grad_blk, lse_blk, delta_blk, query_pos, key_blk, value_blk, key_pos):
    factor = query_blk.shape[2] ** (-0.5)
    scores = (
        jnp.einsum("qhd,khd->hqk", query_blk, key_blk, preferred_element_type=jnp.float32) * factor
    )
    visible = key_pos[None, None, :] <= query_pos[None, :, None]
    probs = jnp.where(visible, jnp.exp(scores - lse_blk[:, :, None]), 0.0)
    probs_low = probs.astype(jnp.bfloat16)
    value_part = jnp.einsum("hqk,qhd->khd", probs_low, grad_blk, preferred_element_type=jnp.float32)
    dprobs = jnp.einsum("qhd,khd->hqk", grad_blk, value_blk, preferred_element_type=jnp.float32)
    dscores = (probs * (dprobs - delta_blk[:, :, None])).astype(jnp.bfloat16)
    query_part = (
        jnp.einsum("hqk,khd->qhd", dscores, key_blk, preferred_element_type=jnp.float32) * factor
    )
    key_part = (
        jnp.einsum("hqk,qhd->khd", dscores, query_blk, preferred_element_type=jnp.float32) * factor
    )
    rows = query_blk.shape[0]
    width = query_blk.shape[1] * query_blk.shape[2]
    return (
        query_part.reshape(rows, width),
        key_part.reshape(key_blk.shape[0], width),
        value_part.reshape(key_blk.shape[0], width),
    )


def on_device(queries, keys, values, out_grad, out_proj, attn_out, log_sum, group_order):
    tokens = queries.shape[1]
    width = queries.shape[2]
    heads = log_sum.shape[1]
    head_size = width // heads
    upstream = out_grad[0]
    attn_full = jnp.dot(
        upstream,
        lax.all_gather(out_proj, "dp", axis=0, tiled=True),
        preferred_element_type=jnp.float32,
    )
    attn_grad = attn_full.astype(jnp.bfloat16)
    grad_blk = attn_grad.reshape(tokens, heads, head_size)
    out_blk = attn_out[0].reshape(tokens, heads, head_size)
    delta = jnp.sum(grad_blk.astype(jnp.float32) * out_blk.astype(jnp.float32), axis=2).T
    lse_own = log_sum[0]
    order = group_order[0]
    per_block = tokens // GROUP
    cycle_size = lax.axis_size("ctx")
    here = lax.axis_index("ctx")

    def positions(device):
        group_ids = lax.dynamic_slice_in_dim(order, device * per_block, per_block)
        offsets = jnp.arange(GROUP, dtype=jnp.int32)
        return (group_ids[:, None] * GROUP + offsets[None, :]).reshape(tokens)

    own_pos = positions(here)
    query_blk = queries[0].reshape(tokens, heads, head_size)
    key_flat = keys[0]
    value_flat = values[0]
    key_blk = key_flat.reshape(tokens, heads, head_size)
    value_blk = value_flat.reshape(tokens, heads, head_size)
    own = pair_grads(query_blk, grad_blk, lse_own, delta, own_pos, key_blk, value_blk, own_pos)
    key_prev, value_prev = shifted((key_flat, value_flat), "ctx", 1)
    prev_pos = positions((here - 1 + cycle_size) % cycle_size)
    cross = pair_grads(
        query_blk,
        grad_blk,
        lse_own,
        delta,
        own_pos,
        key_prev.reshape(tokens, heads, head_size),
        value_prev.reshape(tokens, heads, head_size),
        prev_pos,
    )
    key_back, value_back = shifted((cross[1], cross[2]), "ctx", -1)
    query_total = own[0] + cross[0]
    key_total = own[1] + key_back
    value_total = own[2] + value_back
    return (
        query_total.astype(jnp.bfloat16).reshape(1, tokens, width),
        key_total.astype(jnp.bfloat16).reshape(1, tokens, width),
        value_total.astype(jnp.bfloat16).reshape(1, tokens, width),
    )


def solution(mesh):
    return jax.shard_map(
        on_device,
        mesh=mesh,
        in_specs=(
            P("dp", "ctx", None),
            P("dp", "ctx", None),
            P("dp", "ctx", None),
            P("dp", "ctx", None),
            P("dp", None),
            P("dp", "ctx", None),
            P("dp", None, "ctx"),
            P("dp", None),
        ),
        out_specs=(P("dp", "ctx", None), P("dp", "ctx", None), P("dp", "ctx", None)),
        check_vma=False,
    )
```

profile of v0, /device:TPU:1, one launch (start us, length us, event | category | flops | bytes accessed | tf_op | source)
XLA Modules:
  0.0 186.6 jit_solution(16854233429764616080)
XLA Ops:
  7.2 0.0 copy-start
  7.2 0.0 copy-start.5
  7.2 0.0 all-gather.2.cloned.1.call-start
  7.2 0.7 all-gather.2.cloned.1.call-update
  7.9 2.0 %copy.64 = bf16[1,128,2048]{1,2,0:T(8,128)(2,1)} copy(bf16[1,128,2048]{2,1,0:T(8,128)(2,1)} %param.10) | data formatting | bytes 1048576 | tf_op args[2]
  10.0 4.4 %collective-permute-start.1 = (bf16[128,2048]{0,1:T(8,128)(2,1)}, bf16[128,2048]{0,1:T(8,128)(2,1)}, u32[]{:S(2)}, u32[]{:S(2)}) collective-permute-start(bf16[128,2048]{0,1:T(8,128)(2,1)} %bitcast.7), channel_id=1, source_target_pairs={{0,1},{1,2},{2,3},{3,4},{4,5},{5,6},{6,7},{7,8},{8,9},{9,10},{10,1... | collective-permute-start | bytes 1572872 | tf_op jit(solution)/shard_map/ppermute | solution.py:11
  14.3 1.3 copy.89
  15.6 0.0 copy-start.2
  15.7 3.5 %collective-permute-start = (bf16[128,2048]{0,1:T(8,128)(2,1)S(1)}, bf16[128,2048]{0,1:T(8,128)(2,1)S(1)}, u32[]{:S(2)}, u32[]{:S(2)}) collective-permute-start(bf16[128,2048]{0,1:T(8,128)(2,1)S(1)} %bitcast.70), channel_id=1, source_target_pairs={{0,1},{1,2},{2,3},{3,4},{4,5},{5,6},{6,7},{7,8},{8,9},{9,10},{10,1... | collective-permute-start | bytes 1572872 | tf_op jit(solution)/shard_map/ppermute | solution.py:11
  19.2 0.8 multiply_bitcast_fusion
  20.0 1.1 convert_bitcast_fusion
  21.2 0.1 iota_add_fusion
  21.3 0.1 add.89
  21.3 0.1 add.82
  21.4 1.3 copy.88
  22.7 2.0 %copy.91 = bf16[16,8,16,128]{3,2,1,0:T(8,128)(2,1)} copy(bf16[16,8,16,128]{3,1,2,0:T(8,128)(2,1)} %bitcast.78) | data formatting | bytes 1048576
  24.7 1.3 copy.92
  26.0 0.1 broadcast_compare_fusion
  26.0 0.0 copy-done.5
  26.1 0.5 fusion.10
  26.6 19.5 %collective-permute-done = bf16[128,2048]{0,1:T(8,128)(2,1)S(1)} collective-permute-done((bf16[128,2048]{0,1:T(8,128)(2,1)S(1)}, bf16[128,2048]{0,1:T(8,128)(2,1)S(1)}, u32[]{:S(2)}, u32[]{:S(2)}) %collective-permute-start) | collective-permute-done | bytes 524320 | tf_op jit(solution)/shard_map/ppermute | solution.py:11
  46.1 0.0 copy-start.4
  46.1 1.5 fusion.6
  47.6 57.5 %all-gather.2.cloned.1.call-done = bf16[2048,2048]{1,0:T(8,128)(2,1)} async-done(((bf16[128,2048]{1,0:T(8,128)(2,1)}), bf16[2048,2048]{1,0:T(8,128)(2,1)}) %all-gather.2.cloned.1.call-update) | async-done | bytes 8388624 | tf_op jit(solution)/shard_map/all_gather | solution.py:48
  105.2 0.0 copy-done.4
  105.2 0.0 copy-done
  105.2 4.6 %fusion.15 = bf16[16,8,16,128]{3,1,2,0:T(8,128)(2,1)S(1)} fusion(bf16[2048,2048]{1,0:T(8,128)(2,1)} %all-gather.2.cloned.1.call-done, bf16[1,128,2048]{2,1,0:T(8,128)(2,1)S(1)} %copy-done), kind=kOutput, calls=%fused_computation.23 | convolution fusion | flops 1074003968 | bytes 9437184 | tf_op jit(solution)/shard_map/dot_general | solution.py:46
  109.8 0.0 copy-done.2
  109.8 0.1 copy.90
  109.9 0.5 copy.76
  110.4 1.3 fusion.22
  111.7 2.5 %copy.79 = f32[128,2048]{1,0:T(8,128)} copy(f32[128,2048]{0,1:T(8,128)} %bitcast.74) | data formatting | bytes 2097152 | tf_op jit(solution)/shard_map/reshape | solution.py:36
  114.2 2.5 %fusion.20 = f32[16,128,128]{2,1,0:T(8,128)} fusion(bf16[128,16,128]{0,2,1:T(8,128)(2,1)S(1)} %copy.76, f32[16,128,128]{2,1,0:T(8,128)} %fusion.6), kind=kOutput, calls=%fused_computation.32 | convolution fusion | flops 67371008 | bytes 2621440 | tf_op jit(solution)/shard_map/hqk,qhd->khd/dot_general | solution.py:22
  116.7 2.6 %copy.78 = f32[128,2048]{1,0:T(8,128)} copy(f32[128,2048]{0,1:T(8,128)} %bitcast.75) | data formatting | bytes 2097152 | tf_op jit(solution)/shard_map/reshape | solution.py:36
  119.3 1.6 multiply_reduce_fusion
  120.9 0.1 copy.59
  120.9 0.0 collective-permute-done.1
  120.9 1.9 %fusion.12 = bf16[16,128,128]{2,1,0:T(8,128)(2,1)S(1)} fusion(f32[16,128,128]{2,1,0:T(8,128)} %fusion.6, bf16[128,16,128]{0,2,1:T(8,128)(2,1)S(1)} %copy.76, bf16[128,16,128]{0,2,1:T(8,128)(2,1)} %bitcast.8, f32[16,128]{1,0:T(8,128)S(1)} %copy.59), kind=kOutput, calls=%fused_computation.20 | convolution fusion | flops 67895296 | bytes 2629632 | tf_op jit(solution)/shard_map/qhd,khd->hqk/dot_general | solution.py:23
  122.9 1.5 fusion
  124.4 2.6 %copy.75 = f32[128,16,128]{0,2,1:T(8,128)} copy(f32[128,16,128]{2,0,1:T(8,128)} %fusion) | data formatting | bytes 2097152 | tf_op jit(solution)/shard_map/mul | solution.py:29
  126.9 5.7 %collective-permute-start.2 = (f32[128,2048]{0,1:T(8,128)}, f32[128,2048]{0,1:T(8,128)}, u32[]{:S(2)}, u32[]{:S(2)}) collective-permute-start(f32[128,2048]{0,1:T(8,128)} %bitcast.82), channel_id=1, source_target_pairs={{0,31},{1,0},{2,1},{3,2},{4,3},{5,4},{6,5},{7,6},{8,7},{9,8},{10,9... | collective-permute-start | bytes 3145736 | tf_op jit(solution)/shard_map/ppermute | solution.py:11
  132.6 3.0 %collective-permute-start.3 = (f32[128,2048]{1,0:T(8,128)}, f32[128,2048]{1,0:T(8,128)}, u32[]{:S(2)}, u32[]{:S(2)}) collective-permute-start(f32[128,2048]{1,0:T(8,128)} %copy.78), channel_id=1, source_target_pairs={{0,31},{1,0},{2,1},{3,2},{4,3},{5,4},{6,5},{7,6},{8,7},{9,8},{10,9... | collective-permute-start | bytes 3145736 | tf_op jit(solution)/shard_map/ppermute | solution.py:11
  135.6 1.6 fusion.11
  137.3 0.0 copy-start.1
  137.3 0.8 copy-done.1
  138.1 0.0 copy-start.3
  138.1 1.6 fusion.24
  139.7 1.5 fusion.14
  141.2 0.3 copy.69
  141.5 1.0 copy.80
  142.5 2.6 %fusion.1 = f32[128,16,128]{2,0,1:T(8,128)} fusion(bf16[16,128,128]{2,1,0:T(8,128)(2,1)} %copy-done.1, bf16[128,16,128]{0,2,1:T(8,128)(2,1)S(1)} %bitcast.67), kind=kOutput, calls=%fused_computation.4 | convolution fusion | flops 67371008 | bytes 2097152 | tf_op jit(solution)/shard_map/hqk,qhd->khd/dot_general | solution.py:29
  145.1 1.6 copy.72
  146.6 8.5 %collective-permute-done.2 = f32[128,2048]{0,1:T(8,128)} collective-permute-done((f32[128,2048]{0,1:T(8,128)}, f32[128,2048]{0,1:T(8,128)}, u32[]{:S(2)}, u32[]{:S(2)}) %collective-permute-start.2) | collective-permute-done | bytes 1048608 | tf_op jit(solution)/shard_map/ppermute | solution.py:11
  155.2 1.3 fusion.16
  156.5 1.0 copy.81
  157.5 20.1 %collective-permute-done.3 = f32[128,2048]{1,0:T(8,128)} collective-permute-done((f32[128,2048]{1,0:T(8,128)}, f32[128,2048]{1,0:T(8,128)}, u32[]{:S(2)}, u32[]{:S(2)}) %collective-permute-start.3) | collective-permute-done | bytes 1048608 | tf_op jit(solution)/shard_map/ppermute | solution.py:11
  177.6 0.0 copy-done.3
  177.6 2.1 %fusion.17 = bf16[1,128,2048]{2,1,0:T(8,128)(2,1)} fusion(f32[128,2048]{1,0:T(8,128)S(1)} %copy-done.3, f32[128,2048]{1,0:T(8,128)} %collective-permute-done.3), kind=kLoop, calls=%fused_computation.29 | loop fusion | flops 524288 | bytes 2621440 | tf_op jit(solution)/shard_map/reshape | solution.py:92
Async XLA Ops:
  7.2 98.0 %copy-start = (bf16[1,128,2048]{2,1,0:T(8,128)(2,1)S(1)}, bf16[1,128,2048]{2,1,0:T(8,128)(2,1)}, u32[]{:S(2)}) copy-start(bf16[1,128,2048]{2,1,0:T(8,128)(2,1)} %param.11) | copy-start | bytes 1572868
  7.2 18.9 %copy-start.5 = (f32[1,16,128]{2,1,0:T(8,128)S(1)}, f32[1,16,128]{2,1,0:T(8,128)}, u32[]{:S(2)}) copy-start(f32[1,16,128]{2,1,0:T(8,128)} %param.14) | copy-start | bytes 24580
  7.2 98.0 %all-gather.2.cloned.1.call-start = ((), (), s32[]{:S(2)}) async-start(), calls=%async_computation | async-start | bytes 8912896 | tf_op jit(solution)/shard_map/all_gather | solution.py:48
  10.0 111.0 %collective-permute-start.1 = (bf16[128,2048]{0,1:T(8,128)(2,1)}, bf16[128,2048]{0,1:T(8,128)(2,1)}, u32[]{:S(2)}, u32[]{:S(2)}) collective-permute-start(bf16[128,2048]{0,1:T(8,128)(2,1)} %bitcast.7), channel_id=1, source_target_pairs={{0,1},{1,2},{2,3},{3,4},{4,5},{5,6},{6,7},{7,8},{8,9},{9,10},{10,1... | collective-permute-start | bytes 1572872 | tf_op jit(solution)/shard_map/ppermute | solution.py:11
  15.6 94.2 %copy-start.2 = (bf16[1,128,2048]{1,2,0:T(8,128)(2,1)}, bf16[1,128,2048]{1,2,0:T(8,128)(2,1)S(1)}, u32[]{:S(2)}) copy-start(bf16[1,128,2048]{1,2,0:T(8,128)(2,1)S(1)} %copy.89) | copy-start | bytes 1572868
  15.7 30.5 %collective-permute-start = (bf16[128,2048]{0,1:T(8,128)(2,1)S(1)}, bf16[128,2048]{0,1:T(8,128)(2,1)S(1)}, u32[]{:S(2)}, u32[]{:S(2)}) collective-permute-start(bf16[128,2048]{0,1:T(8,128)(2,1)S(1)} %bitcast.70), channel_id=1, source_target_pairs={{0,1},{1,2},{2,3},{3,4},{4,5},{5,6},{6,7},{7,8},{8,9},{9,10},{10,1... | collective-permute-start | bytes 1572872 | tf_op jit(solution)/shard_map/ppermute | solution.py:11
  46.1 59.0 %copy-start.4 = (bf16[128,2048]{0,1:T(8,128)(2,1)}, bf16[128,2048]{0,1:T(8,128)(2,1)S(1)}, u32[]{:S(2)}) copy-start(bf16[128,2048]{0,1:T(8,128)(2,1)S(1)} %collective-permute-done) | copy-start | bytes 1572868
  126.9 28.2 %collective-permute-start.2 = (f32[128,2048]{0,1:T(8,128)}, f32[128,2048]{0,1:T(8,128)}, u32[]{:S(2)}, u32[]{:S(2)}) collective-permute-start(f32[128,2048]{0,1:T(8,128)} %bitcast.82), channel_id=1, source_target_pairs={{0,31},{1,0},{2,1},{3,2},{4,3},{5,4},{6,5},{7,6},{8,7},{9,8},{10,9... | collective-permute-start | bytes 3145736 | tf_op jit(solution)/shard_map/ppermute | solution.py:11
  132.6 45.0 %collective-permute-start.3 = (f32[128,2048]{1,0:T(8,128)}, f32[128,2048]{1,0:T(8,128)}, u32[]{:S(2)}, u32[]{:S(2)}) collective-permute-start(f32[128,2048]{1,0:T(8,128)} %copy.78), channel_id=1, source_target_pairs={{0,31},{1,0},{2,1},{3,2},{4,3},{5,4},{6,5},{7,6},{8,7},{9,8},{10,9... | collective-permute-start | bytes 3145736 | tf_op jit(solution)/shard_map/ppermute | solution.py:11
  137.3 0.8 copy-start.1
  138.1 39.6 %copy-start.3 = (f32[128,2048]{1,0:T(8,128)S(1)}, f32[128,2048]{1,0:T(8,128)}, u32[]{:S(2)}) copy-start(f32[128,2048]{1,0:T(8,128)} %copy.79) | copy-start | bytes 3145732
Sparse Core Ops, SparseCore 0:
  11.3 93.8 all-gather.1
where the time goes:
time: 188 us; the launch traced here: 187 us
  waiting for transfers between devices  106 us (56%)
  matrix products  21.2 us (11%)
  local copies, waits for them, and re-layouts  21 us (11%)
  starting transfers between devices  16.6 us (9%)
  between operations  14.2 us (8%)
  other arithmetic  7.12 us (4%)
    all_gather x1, waiting for transfers between devices, on_device(): lax.all_gather(out_proj, 'dp', axis=0, tiled=True)  57.5 us
    ppermute x4, waiting for transfers between devices, shifted(): lax.ppermute(array, axis, [(i, (i + by) % size) for i in range(size)])  48.2 us
    ppermute x4, starting transfers between devices, shifted(): lax.ppermute(array, axis, [(i, (i + by) % size) for i in range(size)])  16.6 us
    unnamed x18, local copies, waits for them, and re-layouts  8.2 us
    reshape x2, local copies, waits for them, and re-layouts, pair_grads(): value_part.reshape(key_blk.shape[0], width)  5.09 us
    dot_general x1, matrix products, on_device(): jnp.dot(upstream, lax.all_gather(out_proj, 'dp', axis=0, tiled=True), pre...  4.65 us
    mul x2, local copies, waits for them, and re-layouts, pair_grads(): jnp.einsum('hqk,qhd->khd', dscores, query_blk, preferred_element_type=jnp...  4.11 us
    dot_general x2, matrix products, pair_grads(): jnp.einsum('hqk,qhd->khd', dscores, query_blk, preferred_element_type=jnp...  4.05 us
  transfers between devices with their start and end apart: 5, of which 4 were waited for; matrix products, arithmetic and copies ran while one was open for 22% of the time, Pallas kernels for 0%

commit v1 on v0

--- a/solution.py
+++ b/solution.py
@@ -45,7 +45,9 @@
     upstream = out_grad[0]
     attn_full = jnp.dot(
         upstream,
-        lax.all_gather(out_proj, "dp", axis=0, tiled=True),
+        jnp.concatenate(
+            lax.all_to_all(jnp.stack([out_proj] * lax.axis_size("dp")), "dp", 0, 0), axis=0
+        ),
         preferred_element_type=jnp.float32,
     )
     attn_grad = attn_full.astype(jnp.bfloat16)

time: 188 us -> 224 us (1.19)
  waiting for transfers between devices: 106 us -> 143 us
  between operations: 14.2 us -> 0.85 us
  starting transfers between devices: 16.6 us -> 23.7 us
  matrix products: 21.2 us -> 24.6 us
  local copies, waits for them, and re-layouts: 21 us -> 23.4 us
    all_to_all x0 -> x1, waiting for transfers between devices: none -> 103 us  [on_device(): lax.all_to_all(jnp.stack([out_proj] * lax.axis_size('dp')), 'dp', 0, 0)]
    all_gather x1 -> x0, waiting for transfers between devices: 57.5 us -> none  [on_device(): lax.all_gather(out_proj, 'dp', axis=0, tiled=True)]
    all_to_all x0 -> x1, starting transfers between devices: none -> 11.4 us  [on_device(): lax.all_to_all(jnp.stack([out_proj] * lax.axis_size('dp')), 'dp', 0, 0)]
    ppermute x4, waiting for transfers between devices: 48.2 us -> 40.5 us  [shifted(): lax.ppermute(array, axis, [(i, (i + by) % size) for i in range(size)])]
    another operation x0 -> x1, local copies, waits for them, and re-layouts: none -> 5.41 us  [on_device(): jnp.stack([out_proj] * lax.axis_size('dp'))]
    ppermute x4, starting transfers between devices: 16.6 us -> 12.3 us  [shifted(): lax.ppermute(array, axis, [(i, (i + by) % size) for i in range(size)])]
    unnamed x18 -> x22, local copies, waits for them, and re-layouts: 8.2 us -> 5.27 us
  transfers between devices with their start and end apart: 5 -> 5, of which waited for: 4 -> 4; matrix products, arithmetic and copies ran while one was open for 22% -> 18% of each run, Pallas kernels for 0% -> 0%
where the time goes in v1:
time: 224 us; the launch traced here: 221 us
  waiting for transfers between devices  143 us (64%)
  matrix products  24.6 us (11%)
  starting transfers between devices  23.7 us (11%)
  local copies, waits for them, and re-layouts  23.4 us (10%)
  other arithmetic  5.68 us (3%)
    all_to_all x1, waiting for transfers between devices, on_device(): lax.all_to_all(jnp.stack([out_proj] * lax.axis_size('dp')), 'dp', 0, 0)  103 us
    ppermute x4, waiting for transfers between devices, shifted(): lax.ppermute(array, axis, [(i, (i + by) % size) for i in range(size)])  40.5 us
    ppermute x4, starting transfers between devices, shifted(): lax.ppermute(array, axis, [(i, (i + by) % size) for i in range(size)])  12.3 us
    all_to_all x1, starting transfers between devices, on_device(): lax.all_to_all(jnp.stack([out_proj] * lax.axis_size('dp')), 'dp', 0, 0)  11.4 us
    another operation x1, local copies, waits for them, and re-layouts, on_device(): jnp.stack([out_proj] * lax.axis_size('dp'))  5.41 us
    dot_general x2, matrix products, pair_grads(): jnp.einsum('hqk,khd->qhd', dscores, key_blk, preferred_element_type=jnp.f...  5.35 us
    unnamed x22, local copies, waits for them, and re-layouts  5.27 us
    mul x2, local copies, waits for them, and re-layouts, pair_grads(): jnp.einsum('hqk,qhd->khd', dscores, query_blk, preferred_element_type=jnp...  5.08 us
  transfers between devices with their start and end apart: 5, of which 4 were waited for; matrix products, arithmetic and copies ran while one was open for 18% of the time, Pallas kernels for 0%

profile of v1, /device:TPU:1, one launch (start us, length us, event | category | flops | bytes accessed | tf_op | source)
XLA Modules:
  0.0 221.5 jit_solution(15571913227536469566)
XLA Ops:
  0.6 0.0 copy-start
  0.6 5.4 %stack.2 = bf16[16,128,2048]{2,1,0:T(8,128)(2,1)} broadcast(bf16[128,2048]{1,0:T(8,128)(2,1)} %param.12), dimensions={1,2} | broadcast | bytes 8912896 | tf_op jit(solution)/shard_map/stack | solution.py:49
  6.1 0.0 copy-start.5
  6.1 0.0 copy-start.3
  6.1 0.0 copy-start.7
  6.1 0.0 copy-start.4
  6.1 0.0 copy-start.6
  6.1 11.4 %all-to-all-start = ((bf16[16,128,2048]{2,1,0:T(8,128)(2,1)}), bf16[16,128,2048]{2,1,0:T(8,128)(2,1)}, u32[]{:S(2)}, u32[]{:S(2)}) async-start(bf16[16,128,2048]{2,1,0:T(8,128)(2,1)} %stack.2), calls=%async_computation | async-start | bytes 16777216 | tf_op jit(solution)/shard_map/all_to_all | solution.py:49
  17.5 0.0 copy-done.5
  17.5 0.3 copy.89
  17.8 0.0 copy-start.2
  17.8 1.9 collective-permute-start
  19.7 0.0 copy-done.3
  19.8 1.0 copy.64
  20.8 2.3 %collective-permute-start.1 = (bf16[128,2048]{0,1:T(8,128)(2,1)}, bf16[128,2048]{0,1:T(8,128)(2,1)}, u32[]{:S(2)}, u32[]{:S(2)}) collective-permute-start(bf16[128,2048]{0,1:T(8,128)(2,1)} %bitcast.8), channel_id=1, source_target_pairs={{0,1},{1,2},{2,3},{3,4},{4,5},{5,6},{6,7},{7,8},{8,9},{9,10},{10,1... | collective-permute-start | bytes 1572872 | tf_op jit(solution)/shard_map/ppermute | solution.py:11
  23.1 0.0 copy-done.7
  23.1 0.1 multiply_bitcast_fusion
  23.2 0.0 copy-done.4
  23.2 0.1 convert_bitcast_fusion
  23.3 0.1 iota_add_fusion
  23.3 1.3 copy.88
  24.7 0.1 add.89
  24.7 0.1 add.82
  24.8 0.9 copy.91
  25.7 1.2 copy.92
  26.9 0.1 broadcast_compare_fusion
  27.0 0.0 copy-done.6
  27.0 0.5 fusion.10
  27.6 19.1 %collective-permute-done = bf16[128,2048]{0,1:T(8,128)(2,1)} collective-permute-done((bf16[128,2048]{0,1:T(8,128)(2,1)S(1)}, bf16[128,2048]{0,1:T(8,128)(2,1)}, u32[]{:S(2)}, u32[]{:S(2)}) %collective-permute-start) | collective-permute-done | bytes 524320 | tf_op jit(solution)/shard_map/ppermute | solution.py:11
  46.7 2.6 %fusion.6 = f32[16,128,128]{2,1,0:T(8,128)} fusion(bf16[128,16,128]{0,2,1:T(8,128)(2,1)S(1)} %bitcast.66, bf16[128,16,128]{0,2,1:T(8,128)(2,1)} %bitcast.7, f32[16,128]{1,0:T(8,128)S(1)} %bitcast.84, pred[128,128]{1,0:T(8,128)(4,1)S(1)} %get-tuple-element.9), kind=kOutput, calls=%fused_computation.12 | convolution fusion | flops 67895296 | bytes 2121728 | tf_op jit(solution)/shard_map/qhd,khd->hqk/dot_general | solution.py:17
  49.3 102.7 %all-to-all-done = bf16[16,128,2048]{2,1,0:T(8,128)(2,1)} async-done(((bf16[16,128,2048]{2,1,0:T(8,128)(2,1)}), bf16[16,128,2048]{2,1,0:T(8,128)(2,1)}, u32[]{:S(2)}, u32[]{:S(2)}) %all-to-all-start) | async-done | bytes 8388640 | tf_op jit(solution)/shard_map/all_to_all | solution.py:49
  152.0 0.0 copy-done
  152.0 4.6 %fusion.15 = bf16[16,8,16,128]{3,1,2,0:T(8,128)(2,1)S(1)} fusion(bf16[2048,2048]{1,0:T(8,128)(2,1)} %bitcast.3, bf16[1,128,2048]{2,1,0:T(8,128)(2,1)S(1)} %copy-done), kind=kOutput, calls=%fused_computation.23 | convolution fusion | flops 1074003968 | bytes 9437184 | tf_op jit(solution)/shard_map/dot_general | solution.py:46
  156.7 0.0 copy-done.2
  156.7 0.1 copy.90
  156.8 0.5 copy.76
  157.3 1.6 multiply_reduce_fusion
  158.8 0.1 copy.59
  158.9 1.6 fusion.11
  160.5 0.0 copy-start.1
  160.5 2.7 %fusion.24 = f32[16,128,128]{2,1,0:T(8,128)} fusion(bf16[16,128,128]{2,1,0:T(8,128)(2,1)S(1)} %fusion.11, bf16[128,16,128]{0,2,1:T(8,128)(2,1)} %bitcast.73), kind=kOutput, calls=%fused_computation.42 | convolution fusion | flops 67108864 | bytes 2097152 | tf_op jit(solution)/shard_map/hqk,khd->qhd/dot_general | solution.py:26
  163.2 0.0 collective-permute-done.1
  163.2 0.0 copy-done.1
  163.2 1.9 fusion.12
  165.2 1.5 fusion
  166.7 2.5 %copy.75 = f32[128,16,128]{0,2,1:T(8,128)} copy(f32[128,16,128]{2,0,1:T(8,128)} %fusion) | data formatting | bytes 2097152 | tf_op jit(solution)/shard_map/mul | solution.py:29
  169.2 5.4 %collective-permute-start.2 = (f32[128,2048]{0,1:T(8,128)}, f32[128,2048]{0,1:T(8,128)}, u32[]{:S(2)}, u32[]{:S(2)}) collective-permute-start(f32[128,2048]{0,1:T(8,128)} %bitcast.81), channel_id=1, source_target_pairs={{0,31},{1,0},{2,1},{3,2},{4,3},{5,4},{6,5},{7,6},{8,7},{9,8},{10,9... | collective-permute-start | bytes 3145736 | tf_op jit(solution)/shard_map/ppermute | solution.py:11
  174.7 2.7 %fusion.14 = bf16[128,16,128]{2,0,1:T(8,128)(2,1)} fusion(f32[16,128,128]{2,1,0:T(8,128)} %fusion.24, bf16[16,128,128]{2,1,0:T(8,128)(2,1)S(1)} %fusion.12, bf16[128,16,128]{0,2,1:T(8,128)(2,1)} %bitcast.7), kind=kOutput, calls=%fused_computation.22 | convolution fusion | flops 67895296 | bytes 2621440 | tf_op jit(solution)/shard_map/hqk,khd->qhd/dot_general | solution.py:26
  177.3 1.3 copy.69
  178.6 1.0 copy.80
  179.6 2.5 %fusion.20 = f32[16,128,128]{2,1,0:T(8,128)} fusion(bf16[128,16,128]{0,2,1:T(8,128)(2,1)S(1)} %copy.76, f32[16,128,128]{2,1,0:T(8,128)} %fusion.6), kind=kOutput, calls=%fused_computation.32 | convolution fusion | flops 67371008 | bytes 2621440 | tf_op jit(solution)/shard_map/hqk,qhd->khd/dot_general | solution.py:22
  182.1 2.5 %copy.78 = f32[128,2048]{1,0:T(8,128)} copy(f32[128,2048]{0,1:T(8,128)} %bitcast.76) | data formatting | bytes 2097152 | tf_op jit(solution)/shard_map/reshape | solution.py:36
  184.7 2.6 %collective-permute-start.3 = (f32[128,2048]{1,0:T(8,128)}, f32[128,2048]{1,0:T(8,128)}, u32[]{:S(2)}, u32[]{:S(2)}) collective-permute-start(f32[128,2048]{1,0:T(8,128)} %copy.78), channel_id=1, source_target_pairs={{0,31},{1,0},{2,1},{3,2},{4,3},{5,4},{6,5},{7,6},{8,7},{9,8},{10,9... | collective-permute-start | bytes 3145736 | tf_op jit(solution)/shard_map/ppermute | solution.py:11
  187.3 2.6 %fusion.1 = f32[128,16,128]{2,0,1:T(8,128)} fusion(bf16[16,128,128]{2,1,0:T(8,128)(2,1)} %copy-done.1, bf16[128,16,128]{0,2,1:T(8,128)(2,1)S(1)} %bitcast.68), kind=kOutput, calls=%fused_computation.4 | convolution fusion | flops 67371008 | bytes 2097152 | tf_op jit(solution)/shard_map/hqk,qhd->khd/dot_general | solution.py:29
  189.9 2.5 %copy.72 = f32[128,16,128]{0,2,1:T(8,128)} copy(f32[128,16,128]{2,0,1:T(8,128)} %fusion.1) | data formatting | bytes 2097152 | tf_op jit(solution)/shard_map/mul | solution.py:29
  192.4 1.3 fusion.22
  193.7 1.6 copy.79
  195.3 1.6 collective-permute-done.2
  196.9 1.6 fusion.16
  198.5 1.0 copy.81
  199.5 19.8 %collective-permute-done.3 = f32[128,2048]{1,0:T(8,128)} collective-permute-done((f32[128,2048]{1,0:T(8,128)}, f32[128,2048]{1,0:T(8,128)}, u32[]{:S(2)}, u32[]{:S(2)}) %collective-permute-start.3) | collective-permute-done | bytes 1048608 | tf_op jit(solution)/shard_map/ppermute | solution.py:11
  219.3 2.1 fusion.17
Async XLA Ops:
  0.6 151.4 %copy-start = (bf16[1,128,2048]{2,1,0:T(8,128)(2,1)S(1)}, bf16[1,128,2048]{2,1,0:T(8,128)(2,1)}, u32[]{:S(2)}) copy-start(bf16[1,128,2048]{2,1,0:T(8,128)(2,1)} %param.11) | copy-start | bytes 1572868
  6.1 11.5 %copy-start.5 = (bf16[1,128,2048]{2,1,0:T(8,128)(2,1)S(1)}, bf16[1,128,2048]{2,1,0:T(8,128)(2,1)}, u32[]{:S(2)}) copy-start(bf16[1,128,2048]{2,1,0:T(8,128)(2,1)} %param.9) | copy-start | bytes 1572868
  6.1 13.7 %copy-start.3 = (bf16[1,128,2048]{2,1,0:T(8,128)(2,1)S(1)}, bf16[1,128,2048]{2,1,0:T(8,128)(2,1)}, u32[]{:S(2)}) copy-start(bf16[1,128,2048]{2,1,0:T(8,128)(2,1)} %param.10) | copy-start | bytes 1572868
  6.1 17.0 %copy-start.7 = (s32[1,128]{1,0:T(1,128)S(1)}, s32[1,128]{1,0:T(1,128)}, u32[]{:S(2)}) copy-start(s32[1,128]{1,0:T(1,128)} %param.15) | copy-start | bytes 1540
  6.1 17.1 %copy-start.4 = (bf16[1,128,2048]{2,1,0:T(8,128)(2,1)S(1)}, bf16[1,128,2048]{2,1,0:T(8,128)(2,1)}, u32[]{:S(2)}) copy-start(bf16[1,128,2048]{2,1,0:T(8,128)(2,1)} %param.13) | copy-start | bytes 1572868
  6.1 21.0 %copy-start.6 = (f32[1,16,128]{2,1,0:T(8,128)S(1)}, f32[1,16,128]{2,1,0:T(8,128)}, u32[]{:S(2)}) copy-start(f32[1,16,128]{2,1,0:T(8,128)} %param.14) | copy-start | bytes 24580
  6.1 145.9 %all-to-all-start = ((bf16[16,128,2048]{2,1,0:T(8,128)(2,1)}), bf16[16,128,2048]{2,1,0:T(8,128)(2,1)}, u32[]{:S(2)}, u32[]{:S(2)}) async-start(bf16[16,128,2048]{2,1,0:T(8,128)(2,1)} %stack.2), calls=%async_computation | async-start | bytes 16777216 | tf_op jit(solution)/shard_map/all_to_all | solution.py:49
  17.8 138.8 %copy-start.2 = (bf16[1,128,2048]{1,2,0:T(8,128)(2,1)}, bf16[1,128,2048]{1,2,0:T(8,128)(2,1)S(1)}, u32[]{:S(2)}) copy-start(bf16[1,128,2048]{1,2,0:T(8,128)(2,1)S(1)} %copy.89) | copy-start | bytes 1572868
  17.8 28.9 %collective-permute-start = (bf16[128,2048]{0,1:T(8,128)(2,1)S(1)}, bf16[128,2048]{0,1:T(8,128)(2,1)}, u32[]{:S(2)}, u32[]{:S(2)}) collective-permute-start(bf16[128,2048]{0,1:T(8,128)(2,1)S(1)} %bitcast.71), channel_id=1, source_target_pairs={{0,1},{1,2},{2,3},{3,4},{4,5},{5,6},{6,7},{7,8},{8,9},{9,10},{10,1... | collective-permute-start | bytes 1572872 | tf_op jit(solution)/shard_map/ppermute | solution.py:11
  20.8 142.5 %collective-permute-start.1 = (bf16[128,2048]{0,1:T(8,128)(2,1)}, bf16[128,2048]{0,1:T(8,128)(2,1)}, u32[]{:S(2)}, u32[]{:S(2)}) collective-permute-start(bf16[128,2048]{0,1:T(8,128)(2,1)} %bitcast.8), channel_id=1, source_target_pairs={{0,1},{1,2},{2,3},{3,4},{4,5},{5,6},{6,7},{7,8},{8,9},{9,10},{10,1... | collective-permute-start | bytes 1572872 | tf_op jit(solution)/shard_map/ppermute | solution.py:11
  160.5 2.7 %copy-start.1 = (bf16[16,128,128]{2,1,0:T(8,128)(2,1)}, bf16[16,128,128]{2,1,0:T(8,128)(2,1)S(1)}, u32[]{:S(2)}) copy-start(bf16[16,128,128]{2,1,0:T(8,128)(2,1)S(1)} %fusion.11) | copy-start | bytes 1572868
  169.2 27.7 %collective-permute-start.2 = (f32[128,2048]{0,1:T(8,128)}, f32[128,2048]{0,1:T(8,128)}, u32[]{:S(2)}, u32[]{:S(2)}) collective-permute-start(f32[128,2048]{0,1:T(8,128)} %bitcast.81), channel_id=1, source_target_pairs={{0,31},{1,0},{2,1},{3,2},{4,3},{5,4},{6,5},{7,6},{8,7},{9,8},{10,9... | collective-permute-start | bytes 3145736 | tf_op jit(solution)/shard_map/ppermute | solution.py:11
  184.7 34.7 %collective-permute-start.3 = (f32[128,2048]{1,0:T(8,128)}, f32[128,2048]{1,0:T(8,128)}, u32[]{:S(2)}, u32[]{:S(2)}) collective-permute-start(f32[128,2048]{1,0:T(8,128)} %copy.78), channel_id=1, source_target_pairs={{0,31},{1,0},{2,1},{3,2},{4,3},{5,4},{6,5},{7,6},{8,7},{9,8},{10,9... | collective-permute-start | bytes 3145736 | tf_op jit(solution)/shard_map/ppermute | solution.py:11
